TPU v7x, 256 devices: a whole 4x4x8 slice. The times are simulated.
256 devices in a mesh: head: 16 (over z, core), tail: 16 (over y, x).
Axes of the slice: x: 4, y: 4, z: 8, core: 2. Of those that a mesh axis runs over, the one named last changes fastest.
Arguments:
- head_emb: bfloat16 [131072, 800], P(('head', 'tail')), may hold values from -48 to 48
- head_state: float32 [131072], P(('head', 'tail')), may hold values from 0.01 to 1
- tail_emb: bfloat16 [64, 128, 800], P('tail'), may hold values from -1.5 to 1.5
- tail_state: float32 [64, 128], P('tail'), may hold values from 0.01 to 1
- relation_emb: bfloat16 [1024, 800], replicated, may hold values from -3.5 to 3.5
- head_rows: int32 [1024, 256], P(('head', 'tail')), may hold values from 0 to 511
- relations: int32 [1024, 256], P(('head', 'tail')), may hold values from 0 to 1023
- tail_offsets: int32 [1024, 256], P(('head', 'tail')), may hold values from 0 to 127
- tail_owner: int32 [1024, 1], P(('head', 'tail')), may hold values from 0 to 15; in each aligned block of 4 rows (0 to 3, 4 to 7, ...) at most 2 rows name the same one
- tail_local: int32 [1024], P(('head', 'tail')), may hold values from 0 to 3
- block_count: int32 [256], P(('head', 'tail')), may hold values from 1 to 4, as said below
- neg_blocks: int32 [8], replicated, may hold values from 0 to 63, as said below
Outputs:
- head_new: bfloat16 [131072, 800], P(('head', 'tail'))
- head_state_new: float32 [131072], P(('head', 'tail'))
- tail_new: bfloat16 [64, 128, 800], P('tail')
- tail_state_new: float32 [64, 128], P('tail')
Inputs may be any that keep to these rules, and one draw needn't show every extreme that they name: `tail_owner`: no tail index owns the tail blocks of more than 2 edge block slots of one device, and in some devices one owns exactly 2. `block_count`: some device has all 4 slots live. `neg_blocks`: distinct tail blocks; the last tail block is always among them.
All inputs are finite; a program needn't handle non-finite values.
Results may differ from a plain program's by a relative error of at most 0.0012.
The roundings to bfloat16 on the way count: a program that leaves them out, or rounds other values in their place, can miss the bound.
Values may be sent and summed in bfloat16 or wider, within the bound.
A program may use at most 128 MiB of HBM per device.

v0:
```python
import math
import jax
import jax.numpy as jnp
from jax import lax
from jax.sharding import PartitionSpec as P

LEARN_RATE = 0.3


def complex_product(left, right):
    half_width = left.shape[-1] // 2
    left_re, left_im = (left[..., :half_width], left[..., half_width:])
    right_re, right_im = (right[..., :half_width], right[..., half_width:])
    return jnp.concatenate(
        [left_re * right_re - left_im * right_im, left_re * right_im + left_im * right_re], axis=-1
    )


def conj_product(left, right):
    half_width = left.shape[-1] // 2
    left_re, left_im = (left[..., :half_width], left[..., half_width:])
    right_re, right_im = (right[..., :half_width], right[..., half_width:])
    return jnp.concatenate(
        [left_re * right_re + left_im * right_im, left_im * right_re - left_re * right_im], axis=-1
    )


def row_adagrad(embedding, adagrad_state, gradient):
    state_next = adagrad_state + jnp.mean(gradient * gradient, axis=-1)
    updated = (
        embedding.astype(jnp.float32) - LEARN_RATE * gradient / jnp.sqrt(state_next)[..., None]
    )
    return (updated.astype(jnp.bfloat16), state_next)


def head_sum(tail_grad):
    return lax.psum(tail_grad, "head")


def per_device(
    head_emb,
    head_state,
    tail_emb,
    tail_state,
    relation_emb,
    head_rows,
    relations,
    tail_offsets,
    tail_owner,
    tail_local,
    block_count,
    neg_blocks,
):
    block_total = tail_local.shape[0]
    edge_count = head_rows.shape[1]
    row_width = head_emb.shape[1]
    span_rows = tail_emb.shape[1]
    owned_blocks = tail_emb.shape[0]
    peer_count = lax.axis_size("tail")
    tail_rank = lax.axis_index("tail")
    capacity = max(2, (2 * block_total + peer_count - 1) // peer_count)
    owner_rank = tail_owner[:, 0]
    positions = jnp.arange(block_total, dtype=jnp.int32)
    same_owner = owner_rank[:, None] == owner_rank[None, :]
    earlier = positions[None, :] < positions[:, None]
    slot_index = jnp.sum((same_owner & earlier).astype(jnp.int32), axis=1)
    slot_place = owner_rank * capacity + slot_index
    global_block = owner_rank * owned_blocks + tail_local
    partition = lax.all_gather(tail_emb, "tail", axis=0, tiled=True)
    chosen = jnp.take(partition, global_block, axis=0)
    mine_ids = neg_blocks - tail_rank * owned_blocks
    is_mine = (mine_ids >= 0) & (mine_ids < owned_blocks)
    own_negs = jnp.where(
        is_mine[:, None, None],
        jnp.take(tail_emb, jnp.clip(mine_ids, 0, owned_blocks - 1), axis=0),
        jnp.zeros((), jnp.bfloat16),
    )
    negatives = lax.psum(own_negs.astype(jnp.float32).astype(jnp.bfloat16), "tail").reshape(
        -1, row_width
    )
    total_edges = block_total * edge_count
    flat_rows = head_rows.reshape(-1)
    block_of = jnp.arange(total_edges, dtype=jnp.int32) // edge_count
    live_mask = (block_of < block_count[0]).astype(jnp.float32)
    tail_index = block_of * span_rows + tail_offsets.reshape(-1)
    tail_vectors = jnp.take(chosen.reshape(-1, row_width), tail_index, axis=0)
    relation_vectors = jnp.take(relation_emb, relations.reshape(-1), axis=0)
    head_vectors = jnp.take(head_emb, flat_rows, axis=0)
    query = complex_product(
        head_vectors.astype(jnp.float32), relation_vectors.astype(jnp.float32)
    ).astype(jnp.bfloat16)
    per_group = math.gcd(block_total, max(1, 512 // edge_count))
    group_rows = per_group * edge_count
    group_count = total_edges // group_rows

    def grouped(values):
        return values.reshape((group_count, group_rows) + values.shape[1:])

    def score_group(neg_total, group_items):
        query_rows, tail_rows, live_rows = group_items
        query_float = query_rows.astype(jnp.float32)
        positive = jnp.sum(query_float * tail_rows.astype(jnp.float32), axis=1)
        negative = lax.dot_general(
            query_rows, negatives, (((1,), (1,)), ((), ())), preferred_element_type=jnp.float32
        )
        largest = jnp.maximum(positive, jnp.max(negative, axis=1))
        pos_exp = jnp.exp(positive - largest)
        neg_exp = jnp.exp(negative - largest[:, None])
        denominator = pos_exp + jnp.sum(neg_exp, axis=1)
        pos_grad = (pos_exp / denominator - 1.0) * live_rows
        neg_grad = (neg_exp / denominator[:, None] * live_rows[:, None]).astype(jnp.bfloat16)
        query_grad = pos_grad[:, None] * tail_rows.astype(jnp.float32) + jnp.dot(
            neg_grad, negatives, preferred_element_type=jnp.float32
        )
        tail_part = pos_grad[:, None] * query_float
        neg_total = neg_total + lax.dot_general(
            neg_grad, query_rows, (((0,), (0,)), ((), ())), preferred_element_type=jnp.float32
        )
        return (neg_total, (query_grad, tail_part))

    neg_start = jnp.zeros((negatives.shape[0], row_width), jnp.float32)
    neg_part, (query_grad, tail_part) = lax.scan(
        score_group, neg_start, (grouped(query), grouped(tail_vectors), grouped(live_mask))
    )
    query_grad = query_grad.reshape(total_edges, row_width)
    tail_part = tail_part.reshape(total_edges, row_width)
    head_grad = (
        jnp.zeros(head_emb.shape, jnp.float32)
        .at[flat_rows]
        .add(conj_product(query_grad, relation_vectors.astype(jnp.float32)))
    )
    block_grad = (
        jnp.zeros((block_total * span_rows, row_width), jnp.float32)
        .at[tail_index]
        .add(tail_part)
        .astype(jnp.bfloat16)
    )
    outgoing = (
        jnp.zeros((peer_count * capacity, span_rows, row_width), jnp.bfloat16)
        .at[slot_place]
        .set(block_grad.reshape(block_total, span_rows, row_width))
    )
    outgoing = outgoing.reshape(peer_count, capacity, span_rows, row_width)
    slot_ids = (
        jnp.zeros((peer_count * capacity,), jnp.int32)
        .at[slot_place]
        .set(tail_local)
        .reshape(peer_count, capacity)
    )
    incoming, incoming_ids = (
        lax.all_to_all(outgoing, "tail", split_axis=0, concat_axis=0, tiled=True),
        lax.all_to_all(slot_ids, "tail", split_axis=0, concat_axis=0, tiled=True),
    )
    which_block = (
        incoming_ids.reshape(-1)[:, None] == jnp.arange(owned_blocks, dtype=jnp.int32)[None, :]
    ).astype(jnp.bfloat16)
    tail_grad = lax.dot_general(
        which_block,
        incoming.reshape(peer_count * capacity, span_rows * row_width),
        (((0,), (0,)), ((), ())),
        preferred_element_type=jnp.float32,
    )
    neg_weights = (
        (mine_ids[:, None] == jnp.arange(owned_blocks, dtype=jnp.int32)[None, :]) & is_mine[:, None]
    ).astype(jnp.float32)
    neg_all = lax.psum(neg_part, ("head", "tail"))
    tail_total = head_sum(tail_grad) + lax.dot_general(
        neg_weights,
        neg_all.reshape(neg_weights.shape[0], span_rows * row_width),
        (((0,), (0,)), ((), ())),
        precision=lax.Precision.HIGHEST,
        preferred_element_type=jnp.float32,
    )
    head_updated, head_state_updated = row_adagrad(head_emb, head_state, head_grad)
    tail_updated, tail_state_updated = row_adagrad(
        tail_emb, tail_state, tail_total.reshape(owned_blocks, span_rows, row_width)
    )
    return (head_updated, head_state_updated, tail_updated, tail_state_updated)


def solution(mesh):
    placed = (
        P(("head", "tail"), None),
        P(("head", "tail")),
        P("tail", None, None),
        P("tail", None),
        P(),
        P(("head", "tail"), None),
        P(("head", "tail"), None),
        P(("head", "tail"), None),
        P(("head", "tail"), None),
        P(("head", "tail")),
        P(("head", "tail")),
        P(),
    )
    return jax.shard_map(
        per_device,
        mesh=mesh,
        in_specs=placed,
        out_specs=(
            P(("head", "tail"), None),
            P(("head", "tail")),
            P("tail", None, None),
            P("tail", None),
        ),
        check_vma=False,
    )
```

profile of v0, /device:TPU:1, one launch (start us, length us, event | category | flops | bytes accessed | tf_op | source)
XLA Modules:
  0.0 729.9 jit_solution(752198037437776522)
XLA Ops:
  10.9 7.6 %all-to-all-start = ((s32[16,1,2]{2,1,0:T(1,128)}), s32[16,1,2]{2,1,0:T(1,128)S(1)}, u32[]{:S(2)}, u32[]{:S(2)}) async-start(s32[16,1,2]{2,1,0:T(1,128)} %bitcast.13), calls=%async_computation | async-start | bytes 16384 | tf_op jit(solution)/shard_map/all_to_all | solution.py:152
  21.5 3.8 copy.82
  26.1 3.1 copy.79
  29.3 5.3 gather_fusion.3
  34.5 5.3 gather_fusion
  48.7 62.8 %all-gather.2.cloned.1.call-done = bf16[64,128,800]{1,2,0:T(8,128)(2,1)} async-done(((bf16[4,128,800]{1,2,0:T(8,128)(2,1)}), bf16[64,128,800]{1,2,0:T(8,128)(2,1)}) %all-gather.2.cloned.1.call-update) | async-done | bytes 13107216 | tf_op jit(solution)/shard_map/all_gather | solution.py:69
  111.5 5.4 gather_fusion.2
  119.6 5.3 gather_fusion.4
  124.9 3.3 broadcast_select_fusion
  128.2 3.5 copy.84
  131.6 81.5 %all-reduce.4.cloned.1.call-done = bf16[1024,800]{1,0:T(8,128)(2,1)} async-done(((bf16[1024,800]{1,0:T(8,128)(2,1)}), bf16[1024,800]{1,0:T(8,128)(2,1)}) %all-reduce.4.cloned.1.call-update) | async-done | bytes 1638416 | tf_op jit(solution)/shard_map/psum | solution.py:78
  213.2 30.7 %while.17 = (s32[]{:T(128)}, f32[1024,800]{0,1:T(8,128)}, f32[2,512,800]{1,2,0:T(8,128)}, f32[2,512,800]{1,2,0:T(8,128)}, bf16[2,512,800]{1,2,0:T(8,128)(2,1)S(1...) while((s32[]{:T(128)}, f32[1024,800]{0,1:T(8,128)}, ...), condition=%wide.region_5.7_spmd.clone, body=%wide.region_1.6_spmd.clone.sunk | while | flops 2527675904 | bytes 74365712 | solution.py:122
  213.2 3.0 fusion.55
  223.6 4.5 select_add_fusion.2
  238.4 5.4 select_add_fusion.2
  243.9 4.4 copy.95
  248.2 10.8 %scatter_custom_fusion.2 = f32[512,800]{1,0:T(8,128)S(1)} fusion(s32[1024]{0:T(1024)S(1)} %bitcast.112, f32[1024,800]{1,0:T(8,128)} %bitcast.92, f32[]{:T(128)} %constant.133.clone.1), kind=kCustom, calls=%fused_computation.49 | custom fusion | flops 819200 | bytes 1638912 | tf_op jit(solution)/shard_map/scatter-add | solution.py:135
  261.7 3.6 broadcast_in_dim.108
  268.1 4.6 all-to-all-start.1
  272.8 4.9 copy.92
  277.7 6.1 reshape.276
  287.4 4.4 copy.85
  291.8 75.6 %all-to-all-done.1 = bf16[16,2,128,800]{2,3,1,0:T(8,128)(2,1)} async-done(((bf16[16,2,128,800]{2,3,1,0:T(8,128)(2,1)}), bf16[16,2,128,800]{2,3,1,0:T(8,128)(2,1)}, u32[]{:S(2)}, u32[]{:S(2)}) %all-to-all-start.1) | async-done | bytes 6553632 | tf_op jit(solution)/shard_map/all_to_all | solution.py:151
  367.4 11.0 %copy.91 = bf16[16,2,128,800]{3,2,1,0:T(8,128)(2,1)} copy(bf16[16,2,128,800]{2,3,1,0:T(8,128)(2,1)} %all-to-all-done.1) | data formatting | bytes 13107200 | tf_op jit(solution)/shard_map/all_to_all | solution.py:151
  378.5 13.6 %reshape.275 = bf16[32,102400]{1,0:T(8,128)(2,1)} reshape(bf16[16,2,128,800]{3,2,1,0:T(8,128)(2,1)} %copy.91) | data formatting | bytes 13107200 | tf_op jit(solution)/shard_map/reshape | solution.py:159
  392.1 5.1 fusion.20
  397.3 6.6 multiply_add_fusion
  403.9 10.9 %scatter_custom_fusion = f32[512,800]{1,0:T(8,128)S(1)} fusion(s32[1024]{0:T(1024)S(1)} %bitcast.113, f32[1024,400]{1,0:T(8,128)} %get-tuple-element.225, f32[]{:T(128)} %constant.164, f32[1024,400]{1,0:T(8,128)} %get-tuple-element.224, f32[]{:T(128)} %constant.133.clone.1), kind=kCustom, calls=%fused_computation.32 | custom fusion | flops 1638400 | bytes 4915208 | tf_op jit(solution)/shard_map/scatter-add | solution.py:130
  419.1 172.2 %all-reduce.8.cloned.1.call-done = f32[8,102400]{1,0:T(8,128)} async-done(((f32[8,102400]{1,0:T(8,128)}), f32[8,102400]{1,0:T(8,128)}) %all-reduce.8.cloned.1.call-update) | async-done | bytes 3276816 | tf_op jit(solution)/shard_map/psum | solution.py:166
  591.3 116.5 %all-reduce.6.cloned.1.call-done = f32[4,102400]{1,0:T(4,128)} async-done(((f32[4,102400]{1,0:T(4,128)}), f32[4,102400]{1,0:T(4,128)}) %all-reduce.6.cloned.1.call-update) | async-done | bytes 1638416 | tf_op jit(solution)/shard_map/psum | solution.py:37
  707.9 5.1 broadcast_multiply_fusion
  716.2 3.1 mul.157
  (125 shorter events, 56.6 us)
Async XLA Ops:
  7.2 12.1 %copy-start.3 = (bf16[4,128,800]{1,2,0:T(8,128)(2,1)S(1)}, bf16[4,128,800]{1,2,0:T(8,128)(2,1)}, u32[]{:S(2)}) copy-start(bf16[4,128,800]{1,2,0:T(8,128)(2,1)} %param.18) | copy-start | bytes 2457604
  7.2 104.3 %all-gather.2.cloned.1.call-start = ((), (), s32[]{:S(2)}) async-start(), calls=%async_computation.3 | async-start | bytes 13926400 | tf_op jit(solution)/shard_map/all_gather | solution.py:69
  10.9 257.2 %all-to-all-start = ((s32[16,1,2]{2,1,0:T(1,128)}), s32[16,1,2]{2,1,0:T(1,128)S(1)}, u32[]{:S(2)}, u32[]{:S(2)}) async-start(s32[16,1,2]{2,1,0:T(1,128)} %bitcast.13), calls=%async_computation | async-start | bytes 16384 | tf_op jit(solution)/shard_map/all_to_all | solution.py:152
  18.5 194.7 %all-reduce.4.cloned.1.call-start = ((), (), s32[]{:S(2)}) async-start(), calls=%async_computation.2 | async-start | bytes 3670016 | tf_op jit(solution)/shard_map/psum | solution.py:78
  21.5 3.8 copy-start.12
  21.5 3.9 copy-start.15
  21.5 3.9 copy-start.16
  21.5 3.9 copy-start.9
  26.1 3.1 copy-start.10
  42.4 1.8 copy-start.1
  44.2 3.1 copy-start.11
  45.4 1.9 copy-start.6
  213.2 3.1 copy-start.2
  213.2 3.9 copy-start.17
  216.2 4.1 copy-start
  216.2 2.7 copy-start.7
  220.3 1.8 copy-start.8
  228.1 3.1 copy-start.2
  228.1 3.9 copy-start.17
  231.1 4.1 copy-start
  231.1 2.7 copy-start.7
  235.2 1.8 copy-start.8
  268.1 99.3 %all-to-all-start.1 = ((bf16[16,2,128,800]{2,3,1,0:T(8,128)(2,1)}), bf16[16,2,128,800]{2,3,1,0:T(8,128)(2,1)}, u32[]{:S(2)}, u32[]{:S(2)}) async-start(bf16[16,2,128,800]{2,3,1,0:T(8,128)(2,1)} %bitcast.86), calls=%async_computation.1 | async-start | bytes 13107200 | tf_op jit(solution)/shard_map/all_to_all | solution.py:151
  272.7 318.6 %all-reduce.8.cloned.1.call-start = ((), (), s32[]{:S(2)}) async-start(), calls=%async_computation.5 | async-start | bytes 6553600 | tf_op jit(solution)/shard_map/psum | solution.py:166
  283.7 1.1 copy-start.4
  283.7 424.1 %all-reduce.6.cloned.1.call-start = ((), (), s32[]{:S(2)}) async-start(), calls=%async_computation.4 | async-start | bytes 3276800 | tf_op jit(solution)/shard_map/psum | solution.py:37
  403.9 11.1 %copy-start.13 = (f32[512]{0:T(512)S(1)}, f32[512]{0:T(512)}, u32[]{:S(2)}) copy-start(f32[512]{0:T(512)} %param.17) | copy-start | bytes 6148
  716.1 3.1 copy-start.14
  716.2 3.7 copy-start.5
Sparse Core Ops, SparseCore 0:
  10.4 101.0 all-gather.1
  114.9 98.2 all-reduce.3
  283.9 307.4 all-reduce.7
  593.6 114.2 all-reduce.5
where the time goes:
time: 731 us; the launch traced here: 730 us
  waiting for transfers between devices  509 us (70%)
  local copies, waits for them, and re-layouts  111 us (15%)
  other arithmetic  52.5 us (7%)
  matrix products  29.1 us (4%)
  between operations  14.8 us (2%)
  starting transfers between devices  12.4 us (2%)
    psum x1, waiting for transfers between devices, per_device(): neg_all = lax.psum(neg_part, ('head', 'tail'))  172 us
    psum x1, waiting for transfers between devices, head_sum(): return lax.psum(tail_grad, 'head')  117 us
    psum x1, waiting for transfers between devices, per_device(): lax.psum(own_negs.astype(jnp.float32).astype(jnp.bfloat16), 'tail')  81.5 us
    all_to_all x1, waiting for transfers between devices, per_device(): lax.all_to_all(outgoing, 'tail', split_axis=0, concat_axis=0, tiled=True)  75.6 us
    all_gather x1, waiting for transfers between devices, per_device(): partition = lax.all_gather(tail_emb, 'tail', axis=0, tiled=True)  62.8 us
  transfers between devices with their start and end apart: 6, of which 5 were waited for; matrix products, arithmetic and copies ran while one was open for 23% of the time, Pallas kernels for 0%

commit v1 on v0

--- a/solution.py
+++ b/solution.py
@@ -1,3 +1,4 @@
+import functools
 import math
 import jax
 import jax.numpy as jnp
@@ -5,6 +6,15 @@
 from jax.sharding import PartitionSpec as P
 
 LEARN_RATE = 0.3
+
+
+def show_the_columns(in_array, which_axis):
+    everything = lax.all_to_all(jnp.stack([in_array] * lax.axis_size(which_axis)), which_axis, 0, 0)
+    part_next = jnp.concatenate(everything, 0)
+    return part_next
+
+
+make_plate = functools.partial(show_the_columns, which_axis="tail")
 
 
 def complex_product(left, right):
@@ -66,7 +76,7 @@
     slot_index = jnp.sum((same_owner & earlier).astype(jnp.int32), axis=1)
     slot_place = owner_rank * capacity + slot_index
     global_block = owner_rank * owned_blocks + tail_local
-    partition = lax.all_gather(tail_emb, "tail", axis=0, tiled=True)
+    partition = make_plate(tail_emb)
     chosen = jnp.take(partition, global_block, axis=0)
     mine_ids = neg_blocks - tail_rank * owned_blocks
     is_mine = (mine_ids >= 0) & (mine_ids < owned_blocks)

time: 731 us -> 801 us (1.096)
  waiting for transfers between devices: 509 us -> 563 us
  local copies, waits for them, and re-layouts: 111 us -> 120 us
    all_to_all x0 -> x1, waiting for transfers between devices: none -> 173 us  [show_the_columns(): lax.all_to_all(jnp.stack([in_array] * lax.axis_size(which_axis)), which_a...]
    all_gather x1 -> x0, waiting for transfers between devices: 62.8 us -> none  [per_device(): partition = lax.all_gather(tail_emb, 'tail', axis=0, tiled=True)]
    psum x1, waiting for transfers between devices: 81.5 us -> 26.4 us  [per_device(): lax.psum(own_negs.astype(jnp.float32).astype(jnp.bfloat16), 'tail')]
    another operation x0 -> x1, local copies, waits for them, and re-layouts: none -> 8.4 us  [show_the_columns(): jnp.stack([in_array] * lax.axis_size(which_axis))]
  transfers between devices with their start and end apart: 6 -> 6, of which waited for: 5 -> 5; matrix products, arithmetic and copies ran while one was open for 23% -> 21% of each run, Pallas kernels for 0% -> 0%
where the time goes in v1:
time: 801 us; the launch traced here: 794 us
  waiting for transfers between devices  563 us (70%)
  local copies, waits for them, and re-layouts  120 us (15%)
  other arithmetic  50.1 us (6%)
  matrix products  29 us (4%)
  starting transfers between devices  16.6 us (2%)
  between operations  15 us (2%)
    all_to_all x1, waiting for transfers between devices, show_the_columns(): lax.all_to_all(jnp.stack([in_array] * lax.axis_size(which_axis)), which_a...  173 us
    psum x1, waiting for transfers between devices, per_device(): neg_all = lax.psum(neg_part, ('head', 'tail'))  172 us
    psum x1, waiting for transfers between devices, head_sum(): return lax.psum(tail_grad, 'head')  117 us
    all_to_all x1, waiting for transfers between devices, per_device(): lax.all_to_all(outgoing, 'tail', split_axis=0, concat_axis=0, tiled=True)  75.5 us
    psum x1, waiting for transfers between devices, per_device(): lax.psum(own_negs.astype(jnp.float32).astype(jnp.bfloat16), 'tail')  26.4 us
  transfers between devices with their start and end apart: 6, of which 5 were waited for; matrix products, arithmetic and copies ran while one was open for 21% of the time, Pallas kernels for 0%

profile of v1, /device:TPU:1, one launch (start us, length us, event | category | flops | bytes accessed | tf_op | source)
XLA Modules:
  0.0 793.6 jit_solution(10043907354034907498)
XLA Ops:
  7.2 8.4 %stack.2 = bf16[16,4,128,800]{2,3,1,0:T(8,128)(2,1)} broadcast(bf16[4,128,800]{1,2,0:T(8,128)(2,1)} %param.18), dimensions={1,2,3} | broadcast | bytes 13926400 | tf_op jit(solution)/shard_map/stack | solution.py:12
  15.6 7.7 all-to-all-start
  25.7 3.8 copy.117
  33.3 5.3 gather_fusion.3
  38.6 5.3 gather_fusion
  54.3 172.6 %all-to-all-done = bf16[16,4,128,800]{2,3,1,0:T(8,128)(2,1)} async-done(((bf16[16,4,128,800]{2,3,1,0:T(8,128)(2,1)}), bf16[16,4,128,800]{2,3,1,0:T(8,128)(2,1)}, u32[]{:S(2)}, u32[]{:S(2)}) %all-to-all-start) | async-done | bytes 13107232 | tf_op jit(solution)/shard_map/all_to_all | solution.py:12
  226.9 3.9 all-to-all-start.1
  230.8 5.4 gather_fusion.2
  238.9 5.3 gather_fusion.4
  244.2 3.1 broadcast_select_fusion
  247.3 3.5 copy.120
  250.8 26.4 %all-reduce.4.cloned.1.call-done = bf16[1024,800]{1,0:T(8,128)(2,1)} async-done(((bf16[1024,800]{1,0:T(8,128)(2,1)}), bf16[1024,800]{1,0:T(8,128)(2,1)}) %all-reduce.4.cloned.1.call-update) | async-done | bytes 1638416 | tf_op jit(solution)/shard_map/psum | solution.py:88
  277.1 30.4 %while.17 = (s32[]{:T(128)}, f32[1024,800]{0,1:T(8,128)}, f32[2,512,800]{1,2,0:T(8,128)}, f32[2,512,800]{1,2,0:T(8,128)}, bf16[2,512,800]{1,2,0:T(8,128)(2,1)S(1...) while((s32[]{:T(128)}, f32[1024,800]{0,1:T(8,128)}, ...), condition=%wide.region_5.7_spmd.clone, body=%wide.region_1.6_spmd.clone.sunk | while | flops 2527675904 | bytes 74365712 | solution.py:132
  287.5 4.4 select_add_fusion.2
  302.2 5.4 select_add_fusion.2
  307.6 4.4 copy.132
  311.9 10.7 %scatter_custom_fusion.2 = f32[512,800]{1,0:T(8,128)S(1)} fusion(s32[1024]{0:T(1024)S(1)} %bitcast.113, f32[1024,800]{1,0:T(8,128)} %bitcast.93, f32[]{:T(128)} %constant.133.clone.1), kind=kCustom, calls=%fused_computation.49 | custom fusion | flops 819200 | bytes 1638912 | tf_op jit(solution)/shard_map/scatter-add | solution.py:145
  325.2 3.6 broadcast_in_dim.108
  331.6 4.6 all-to-all-start.2
  336.4 4.9 copy.128
  341.3 5.9 reshape.282
  351.0 4.4 copy.121
  355.4 75.5 %all-to-all-done.2 = bf16[16,2,128,800]{2,3,1,0:T(8,128)(2,1)} async-done(((bf16[16,2,128,800]{2,3,1,0:T(8,128)(2,1)}), bf16[16,2,128,800]{2,3,1,0:T(8,128)(2,1)}, u32[]{:S(2)}, u32[]{:S(2)}) %all-to-all-start.2) | async-done | bytes 6553632 | tf_op jit(solution)/shard_map/all_to_all | solution.py:161
  431.0 11.0 %copy.127 = bf16[16,2,128,800]{3,2,1,0:T(8,128)(2,1)} copy(bf16[16,2,128,800]{2,3,1,0:T(8,128)(2,1)} %all-to-all-done.2) | data formatting | bytes 13107200 | tf_op jit(solution)/shard_map/all_to_all | solution.py:161
  442.0 13.6 %reshape.281 = bf16[32,102400]{1,0:T(8,128)(2,1)} reshape(bf16[16,2,128,800]{3,2,1,0:T(8,128)(2,1)} %copy.127) | data formatting | bytes 13107200 | tf_op jit(solution)/shard_map/reshape | solution.py:169
  455.6 5.1 fusion.20
  460.8 6.6 multiply_add_fusion
  467.4 11.1 %scatter_custom_fusion = f32[512,800]{1,0:T(8,128)S(1)} fusion(s32[1024]{0:T(1024)S(1)} %bitcast.114, f32[1024,400]{1,0:T(8,128)} %get-tuple-element.249, f32[]{:T(128)} %constant.164, f32[1024,400]{1,0:T(8,128)} %get-tuple-element.248, f32[]{:T(128)} %constant.133.clone.1), kind=kCustom, calls=%fused_computation.32 | custom fusion | flops 1638400 | bytes 4915208 | tf_op jit(solution)/shard_map/scatter-add | solution.py:140
  482.8 171.9 %all-reduce.8.cloned.1.call-done = f32[8,102400]{1,0:T(8,128)} async-done(((f32[8,102400]{1,0:T(8,128)}), f32[8,102400]{1,0:T(8,128)}) %all-reduce.8.cloned.1.call-update) | async-done | bytes 3276816 | tf_op jit(solution)/shard_map/psum | solution.py:176
  654.7 116.7 %all-reduce.6.cloned.1.call-done = f32[4,102400]{1,0:T(4,128)} async-done(((f32[4,102400]{1,0:T(4,128)}), f32[4,102400]{1,0:T(4,128)}) %all-reduce.6.cloned.1.call-update) | async-done | bytes 1638416 | tf_op jit(solution)/shard_map/psum | solution.py:47
  771.4 5.1 broadcast_multiply_fusion
  779.7 3.1 mul.157
  (127 shorter events, 59.7 us)
Async XLA Ops:
  15.6 7.8 copy-start.15
  15.6 7.9 copy-start.3
  15.6 211.3 %all-to-all-start = ((bf16[16,4,128,800]{2,3,1,0:T(8,128)(2,1)}), bf16[16,4,128,800]{2,3,1,0:T(8,128)(2,1)}, u32[]{:S(2)}, u32[]{:S(2)}) async-start(bf16[16,4,128,800]{2,3,1,0:T(8,128)(2,1)} %stack.2), calls=%async_computation | async-start | bytes 26214400 | tf_op jit(solution)/shard_map/all_to_all | solution.py:12
  23.3 253.8 %all-reduce.4.cloned.1.call-start = ((), (), s32[]{:S(2)}) async-start(), calls=%async_computation.3 | async-start | bytes 3670016 | tf_op jit(solution)/shard_map/psum | solution.py:88
  25.7 3.8 copy-start.9
  29.5 0.7 copy-start.12
  30.2 3.1 copy-start.10
  46.4 1.8 copy-start.1
  48.3 2.4 copy-start.11
  48.3 3.1 copy-start.17
  48.3 3.3 copy-start.16
  49.5 3.4 copy-start.6
  226.9 104.6 %all-to-all-start.1 = ((s32[16,1,2]{2,1,0:T(1,128)}), s32[16,1,2]{2,1,0:T(1,128)S(1)}, u32[]{:S(2)}, u32[]{:S(2)}) async-start(s32[16,1,2]{2,1,0:T(1,128)} %bitcast.14), calls=%async_computation.1 | async-start | bytes 16384 | tf_op jit(solution)/shard_map/all_to_all | solution.py:162
  277.1 3.1 copy-start.2
  277.1 3.9 copy-start.18
  280.2 4.1 copy-start
  280.2 2.7 copy-start.7
  284.3 1.7 copy-start.8
  291.9 3.1 copy-start.2
  291.9 3.9 copy-start.18
  294.9 4.1 copy-start
  295.0 2.7 copy-start.7
  299.1 1.7 copy-start.8
  331.6 99.4 %all-to-all-start.2 = ((bf16[16,2,128,800]{2,3,1,0:T(8,128)(2,1)}), bf16[16,2,128,800]{2,3,1,0:T(8,128)(2,1)}, u32[]{:S(2)}, u32[]{:S(2)}) async-start(bf16[16,2,128,800]{2,3,1,0:T(8,128)(2,1)} %bitcast.87), calls=%async_computation.2 | async-start | bytes 13107200 | tf_op jit(solution)/shard_map/all_to_all | solution.py:161
  336.2 318.5 %all-reduce.8.cloned.1.call-start = ((), (), s32[]{:S(2)}) async-start(), calls=%async_computation.5 | async-start | bytes 6553600 | tf_op jit(solution)/shard_map/psum | solution.py:176
  347.2 1.1 copy-start.4
  347.3 424.1 %all-reduce.6.cloned.1.call-start = ((), (), s32[]{:S(2)}) async-start(), calls=%async_computation.4 | async-start | bytes 3276800 | tf_op jit(solution)/shard_map/psum | solution.py:47
  467.4 11.3 %copy-start.13 = (f32[512]{0:T(512)S(1)}, f32[512]{0:T(512)}, u32[]{:S(2)}) copy-start(f32[512]{0:T(512)} %param.17) | copy-start | bytes 6148
  779.7 3.1 copy-start.14
  779.7 3.7 copy-start.5
Sparse Core Ops, SparseCore 0:
  29.6 247.4 all-reduce.3
  347.4 307.2 all-reduce.7
  657.1 114.2 all-reduce.5
